TPU v7x, 1024 devices: a whole 4x8x16 slice. The times are simulated.
1024 devices in a mesh: member: 16 (over y, core), space: 64 (over z, x).
Axes of the slice: x: 4, y: 8, z: 16, core: 2. Of those that a mesh axis runs over, the one named last changes fastest.
Arguments:
- ensemble: float32 [256, 32, 16384], P('member', None, 'space'), may hold values from -6 to 6
- obs_weight: float32 [32, 65536], P(None, 'space'), may hold values from -1 to 1
- obs_value: float32 [65536], P('space'), may hold values from -6 to 6
- obs_rinv: float32 [65536], P('space'), may hold values from 0.5 to 4
- obs_column: int32 [65536], P('space'), may hold values from 0 to 255
- set_rows: int32 [1024, 512], P('space'), may hold values from 0 to 1023
- set_count: int32 [1024], P('space'), may hold values from 128 to 512, as said below
- neighbour: int32 [4, 16384], P(None, 'space'), may hold values from 0 to 15
- interp_weight: float32 [4, 16384], P(None, 'space'), may hold values from 0.1 to 1
Outputs:
- analysed: float32 [256, 32, 16384], P('member', None, 'space')
Inputs may be any that keep to these rules, and one draw needn't show every extreme that they name: `set_rows`: a row among the 1024 observations of the space index that owns the coarse point; coarse point j is owned by space index j // (member count). `set_count`: rows of a local set at or past its count are padding; some coarse point has the full 512 rows in every draw. `obs_column`: a column among the 256 columns of the space index that holds the observation. `neighbour`: a coarse point among those owned by the column's own space index, numbered from 0.
All inputs are finite; a program needn't handle non-finite values.
Results may differ from a plain program's by a relative error of at most 0.0035.
Values may be sent and summed in bfloat16 or wider, within the bound.
No kernel may reach another device: no remote copies, remote signals or barrier semaphores. Data moves between devices by JAX's collectives and lax.ppermute only.
A program may use at most 32 MiB of HBM per device.

v0:
```python
import jax
import jax.numpy as jnp
from jax import lax
from jax.experimental import pallas as pl
from jax.experimental.pallas import tpu as pltpu
from jax.sharding import PartitionSpec as P


NS_ITERS = 5
F32 = jnp.float32
BF16 = jnp.bfloat16
VMEM = pl.BlockSpec(memory_space=pltpu.VMEM)
SMEM = pl.BlockSpec(memory_space=pltpu.SMEM)


def limit(mib):
    return pltpu.CompilerParams(vmem_limit_bytes=mib << 20)


def split(x):
    hi = x.astype(BF16)
    return hi, (x - hi.astype(F32)).astype(BF16)


def dot(a, b):
    return jnp.dot(a, b, preferred_element_type=F32)


def dot_nt(a, b):
    return lax.dot_general(a, b, (((1,), (1,)), ((), ())), preferred_element_type=F32)


def mm(a, b):
    return dot(a[0], b[0]) + dot(a[0], b[1]) + dot(a[1], b[0])


def pack_kernel(ens, out):
    for v in range(out.shape[0]):
        out[v] = ens[:, v, :].astype(BF16)


def observe_kernel(ens, weight, column, out):
    members, nv, cols = ens.shape
    n_obs = weight.shape[1]
    hi, lo = split(ens[...].reshape(members * nv, cols))
    step = 256
    for start in range(0, n_obs, step):
        at = pl.ds(start, step)
        onehot = (
            lax.broadcasted_iota(jnp.int32, (cols, step), 0) == column[:, at]
        ).astype(F32).astype(BF16)
        picked = dot(hi, onehot) + dot(lo, onehot)
        seen = jnp.sum(picked.reshape(members, nv, step) * weight[:, at][None], axis=1)
        seen = seen.astype(BF16)
        for chip in range(out.shape[0]):
            out[chip, :, at] = seen


def transform_kernel(where, mine, theirs, value, rinv, rows, counts, out, obs, scaled):
    chips, per, n_obs = mine.shape
    size = chips * 2 * per
    me, core = where[0], where[1]
    for chip in range(chips):
        obs[pl.ds(pl.multiple_of(2 * per * chip + per * core, per), per), :] = mine[chip]
        obs[pl.ds(pl.multiple_of(2 * per * chip + per * (1 - core), per), per), :] = theirs[chip]
    picks = rows[pl.ds(me, 1), :]
    mine_only = lax.broadcasted_iota(jnp.int32, counts.shape, 1) == me
    count = jnp.sum(jnp.where(mine_only, counts[...].astype(F32), 0.0), axis=1, keepdims=True)
    live = lax.broadcasted_iota(jnp.int32, picks.shape, 1).astype(F32) < count
    picks = jnp.where(live, picks, -1)
    tiles = n_obs // 128
    coarse = lax.broadcasted_iota(jnp.int32, (tiles, picks.shape[1]), 0) == (picks >> 7)
    fine = lax.broadcasted_iota(jnp.int32, (128, picks.shape[1]), 0) == (picks & 127)
    times = dot_nt(coarse.astype(F32).astype(BF16), fine.astype(F32).astype(BF16))
    root = jnp.sqrt(times * rinv[...])
    for tile in range(tiles):
        at = pl.ds(128 * tile, 128)
        part = obs[:, at].astype(F32)
        mean = jnp.sum(part, axis=0, keepdims=True) * (1.0 / size)
        w = root[tile : tile + 1, :]
        z = w * (value[tile : tile + 1, :] - mean)
        hi, lo = split((part - mean) * w)
        scaled[0, :size, at] = hi
        scaled[1, :size, at] = lo
        hi, lo = split(jnp.broadcast_to(z, (16, 128)))
        scaled[0, size:, at] = hi
        scaled[1, size:, at] = lo
    hi, lo = scaled[0], scaled[1]
    gram = dot_nt(hi, hi[:size]) + dot_nt(hi, lo[:size]) + dot_nt(lo, hi[:size])
    drive = gram[size:]
    diag = lax.broadcasted_iota(jnp.int32, (size, size), 0) == lax.broadcasted_iota(jnp.int32, (size, size), 1)
    eye = diag.astype(F32)
    posterior = gram[:size] + (size - 1.0) * eye
    squares = jnp.sum(jnp.sum(posterior * posterior, axis=0, keepdims=True), axis=1, keepdims=True)
    inv_norm = lax.rsqrt(squares)
    inv_norm = inv_norm * (1.5 - 0.5 * squares * inv_norm * inv_norm)
    product = posterior * inv_norm
    inverse = None
    for turn in range(NS_ITERS):
        ns_step = 1.5 * eye - 0.5 * product
        s = split(ns_step)
        if turn == 0:
            inverse = ns_step
        else:
            inverse = mm(s, split(inverse))
        if turn < NS_ITERS - 1:
            product = mm(s, split(mm(s, split(product))))
    z = split(inverse)
    mean_weight = mm(split(mm(split(drive), z)), z) * inv_norm
    final = inverse * jnp.sqrt((size - 1.0) * inv_norm) + mean_weight[0:1, :]
    final = final.astype(BF16)
    for to in range(2 * chips):
        out[to] = final[per * to : per * (to + 1)]


def apply_kernel(where, trans, neighbour, interp, *refs):
    blocks, (out, lhs) = refs[:-2], refs[-2:]
    points, per, size = trans.shape
    nv, cols = out.shape[1:]
    core, chip = where[1], where[2]
    chips = size // (2 * per)
    raw = interp[...]
    norm = raw / jnp.sum(raw, axis=0, keepdims=True)
    near = neighbour[...]
    point = lax.broadcasted_iota(jnp.int32, (points, cols), 0)
    pointwise = jnp.zeros((points, cols), F32)
    for b in range(raw.shape[0]):
        pointwise = pointwise + jnp.where(point == near[b : b + 1], norm[b : b + 1], 0.0)
    flat = trans[...].reshape(points * per, size)
    sums = jnp.sum(flat.astype(F32), axis=1, keepdims=True)
    rest = jnp.ones((per, cols), F32)
    for m in range(points):
        rest = rest - sums[per * m : per * (m + 1)] * pointwise[m : m + 1]
    lane = lax.broadcasted_iota(jnp.int32, (1, size), 1)
    column = lane % per
    ahead = 2 * core - 1
    for place, (_, _, steps, other) in enumerate(slabs()):
        src = lax.rem(chip + ahead * steps + chips, chips)
        start = per * (2 * src + (1 - core if other else core))
        column = column + jnp.where(lane // per == place, start, 0)
    shuffle = (lax.broadcasted_iota(jnp.int32, (size, size), 0) == column).astype(F32).astype(BF16)
    lhs[: points * per] = dot(flat, shuffle).astype(BF16)
    lhs[points * per :] = jnp.full((16, size), 1.0 / size, BF16)
    for v in range(nv):
        states = jnp.concatenate(
            [blocks[which][v] if index is None else blocks[which][index, v] for which, index, _, _ in slabs()], axis=0
        )
        res = dot(lhs[...], states)
        total = res[points * per : points * per + 1] * rest
        for m in range(points):
            total = total + res[per * m : per * (m + 1)] * pointwise[m : m + 1]
        out[:, v, :] = total


def slabs():
    for hop in range(4):
        yield hop, 0, hop, False
        yield hop, 1, hop, True
    for hop in (1, 2, 3):
        yield 3 + hop, 0, -hop, True
        yield 3 + hop, 1, -hop, False
    yield 7, None, 4, False
    yield 8, None, 4, True


def permute(value, pairs):
    return lax.ppermute(value, "member", pairs)


def analysis(ensemble, obs_weight, obs_value, obs_rinv, obs_column, set_rows, set_count, neighbour, interp_weight):
    count = lax.axis_size("member")
    chips = count // 2
    me = lax.axis_index("member").astype(jnp.int32)
    core = me % 2
    where = jnp.stack([me, core, me // 2])
    per, nv, cols = ensemble.shape
    n_obs = obs_column.shape[0]
    swap = [(i, i ^ 1) for i in range(count)]
    same_core = [[2 * y + c for y in range(chips)] for c in range(2)]

    def along(hops):
        return [(2 * y + c, 2 * ((y + (hops if c else -hops) * -1) % chips) + c) for y in range(chips) for c in range(2)]

    mine = pl.pallas_call(
        pack_kernel,
        out_shape=jax.ShapeDtypeStruct((nv, per, cols), BF16),
        in_specs=[VMEM],
        out_specs=VMEM,
        compiler_params=limit(4),
        name="pack",
    )(ensemble)
    theirs = permute(mine, swap)
    own = jnp.stack([mine, theirs])
    first = permute(own, along(1))
    second = permute(first, along(1))
    third = permute(second, along(1))
    far = permute(first[0], along(3))
    first_too = permute(first, swap)
    second_too = permute(second, swap)
    third_too = permute(third, swap)
    far_too = permute(far, swap)
    blocks = [own, first, second, third, first_too, second_too, third_too, far, far_too]

    seen = pl.pallas_call(
        observe_kernel,
        out_shape=jax.ShapeDtypeStruct((chips, per, n_obs), BF16),
        in_specs=[VMEM] * 3,
        out_specs=VMEM,
        compiler_params=limit(8),
        name="observe",
    )(ensemble, obs_weight, obs_column.reshape(1, n_obs))
    seen = lax.all_to_all(seen, "member", 0, 0, axis_index_groups=same_core, tiled=True)
    seen_too = permute(seen, swap)

    trans = pl.pallas_call(
        transform_kernel,
        out_shape=jax.ShapeDtypeStruct((count, per, count * per), BF16),
        in_specs=[SMEM] + [VMEM] * 6,
        out_specs=VMEM,
        scratch_shapes=[
            pltpu.VMEM((count * per, n_obs), BF16),
            pltpu.VMEM((2, count * per + 16, n_obs), BF16),
        ],
        compiler_params=limit(8),
        name="transform",
    )(
        where,
        seen,
        seen_too,
        obs_value.reshape(n_obs // 128, 128),
        obs_rinv.reshape(n_obs // 128, 128),
        set_rows,
        set_count.reshape(1, count),
    )
    trans = lax.all_to_all(trans, "member", 0, 0, tiled=True)

    return pl.pallas_call(
        apply_kernel,
        out_shape=jax.ShapeDtypeStruct((per, nv, cols), F32),
        in_specs=[SMEM] + [VMEM] * (3 + len(blocks)),
        out_specs=VMEM,
        scratch_shapes=[
            pltpu.VMEM((count * per + 16, count * per), BF16),
        ],
        compiler_params=limit(4),
        name="apply",
    )(where, trans, neighbour, interp_weight, *blocks)


def solution(mesh):
    placed = (
        P("member", None, "space"),
        P(None, "space"),
        P("space"),
        P("space"),
        P("space"),
        P("space", None),
        P("space"),
        P(None, "space"),
        P(None, "space"),
    )
    return jax.shard_map(
        analysis, mesh=mesh, in_specs=placed, out_specs=P("member", None, "space"), check_vma=False
    )
```

profile of v0, /device:TPU:1, one launch (start us, length us, event | category | flops | bytes accessed | tf_op | source)
XLA Modules:
  0.0 97.5 jit_solution(7127689155079365260)
XLA Ops:
  0.0 0.0 copy-start
  0.0 1.0 %copy-done = f32[16,32,256]{2,1,0:T(8,128)S(1)} copy-done((f32[16,32,256]{2,1,0:T(8,128)S(1)}, f32[16,32,256]{2,1,0:T(8,128)}, u32[]{:S(2)}) %copy-start) | copy-done | bytes 524312
  1.0 0.5 pack.1
  1.6 16.0 %collective-permute-start.1 = (bf16[32,16,256]{2,1,0:T(8,128)(2,1)S(1)}, bf16[32,16,256]{2,1,0:T(8,128)(2,1)S(1)}, u32[]{:S(2)}, u32[]{:S(2)}) collective-permute-start(bf16[32,16,256]{2,1,0:T(8,128)(2,1)S(1)} %pack.1), channel_id=1, source_target_pairs={{0,64},{64,0},{128,192},{192,128},{256,320},{320,256},{384,448},{4... | collective-permute-start | bytes 786440 | tf_op jit(solution)/shard_map/ppermute | solution.py:167
  17.6 1.1 %collective-permute-done.1 = bf16[32,16,256]{2,1,0:T(8,128)(2,1)S(1)} collective-permute-done((bf16[32,16,256]{2,1,0:T(8,128)(2,1)S(1)}, bf16[32,16,256]{2,1,0:T(8,128)(2,1)S(1)}, u32[]{:S(2)}, u32[]{:S(2)}) %collective-permute-start.1) | collective-permute-done | bytes 262176 | tf_op jit(solution)/shard_map/ppermute | solution.py:167
  18.7 0.0 copy-start.1
  18.7 0.0 copy-start.2
  18.7 0.0 copy-start.4
  18.7 0.1 pad_maximum_fusion.refs_0_
  18.8 2.1 %collective-permute-start.2 = (bf16[2,32,16,256]{3,2,1,0:T(8,128)(2,1)S(1)}, bf16[2,32,16,256]{3,2,1,0:T(8,128)(2,1)S(1)}, u32[]{:S(2)}, u32[]{:S(2)}) collective-permute-start(bf16[2,32,16,256]{3,2,1,0:T(8,128)(2,1)S(1)} %pad_maximum_fusion.refs_0_), channel_id=1, source_target_pairs={{0,128},{64,960},{128,256},{192,64},{256,384},{320,192},{384,512},... | collective-permute-start | bytes 1572872 | tf_op jit(solution)/shard_map/ppermute | solution.py:167
  20.9 8.3 %collective-permute-done.2.refs_1_ = bf16[2,32,16,256]{3,2,1,0:T(8,128)(2,1)S(1)} collective-permute-done((bf16[2,32,16,256]{3,2,1,0:T(8,128)(2,1)S(1)}, bf16[2,32,16,256]{3,2,1,0:T(8,128)(2,1)S(1)}, u32[]{:S(2)}, u32[]{:S(2)}) %collective-permute-start.2) | collective-permute-done | bytes 524320 | tf_op jit(solution)/shard_map/ppermute | solution.py:167
  29.1 2.8 %collective-permute-start.3 = (bf16[2,32,16,256]{3,2,1,0:T(8,128)(2,1)S(1)}, bf16[2,32,16,256]{3,2,1,0:T(8,128)(2,1)S(1)}, u32[]{:S(2)}, u32[]{:S(2)}) collective-permute-start(bf16[2,32,16,256]{3,2,1,0:T(8,128)(2,1)S(1)} %collective-permute-done.2.refs_1_), channel_id=1, source_target_pairs={{0,128},{64,960},{128,256},{192,64},{256,384},{320,192},{384,512},... | collective-permute-start | bytes 1572872 | tf_op jit(solution)/shard_map/ppermute | solution.py:167
  32.0 7.4 %collective-permute-done.3.refs_2_ = bf16[2,32,16,256]{3,2,1,0:T(8,128)(2,1)S(1)} collective-permute-done((bf16[2,32,16,256]{3,2,1,0:T(8,128)(2,1)S(1)}, bf16[2,32,16,256]{3,2,1,0:T(8,128)(2,1)S(1)}, u32[]{:S(2)}, u32[]{:S(2)}) %collective-permute-start.3) | collective-permute-done | bytes 524320 | tf_op jit(solution)/shard_map/ppermute | solution.py:167
  39.4 3.7 %collective-permute-start.4 = (bf16[2,32,16,256]{3,2,1,0:T(8,128)(2,1)S(1)}, bf16[2,32,16,256]{3,2,1,0:T(8,128)(2,1)S(1)}, u32[]{:S(2)}, u32[]{:S(2)}) collective-permute-start(bf16[2,32,16,256]{3,2,1,0:T(8,128)(2,1)S(1)} %collective-permute-done.3.refs_2_), channel_id=1, source_target_pairs={{0,128},{64,960},{128,256},{192,64},{256,384},{320,192},{384,512},... | collective-permute-start | bytes 1572872 | tf_op jit(solution)/shard_map/ppermute | solution.py:167
  43.1 0.0 copy-done.1
  43.1 0.0 copy-done.2
  43.1 0.0 copy-done.4
  43.1 1.5 %observe.1 = bf16[8,16,1024]{2,1,0:T(8,128)(2,1)} custom-call(f32[16,32,256]{2,1,0:T(8,128)S(1)} %copy-done.1, f32[32,1024]{1,0:T(8,128)S(1)} %copy-done.2, s32[1,1024]{1,0:T(1,128)S(1)} %bitcast.12), custom_call_target="tpu_custom_call" | custom-call | tf_op jit(solution)/shard_map/observe/pallas_call | solution.py:204
  44.6 3.4 %all-to-all-start = ((bf16[8,16,1024]{2,1,0:T(8,128)(2,1)}), bf16[8,16,1024]{2,1,0:T(8,128)(2,1)S(1)}, u32[]{:S(2)}, u32[]{:S(2)}) async-start(bf16[8,16,1024]{2,1,0:T(8,128)(2,1)} %observe.1), calls=%async_computation | async-start | bytes 524288 | tf_op jit(solution)/shard_map/all_to_all | solution.py:212
  48.0 0.7 slice_bitcast_fusion
  48.8 6.4 %collective-permute-start.8 = (bf16[32,16,256]{2,1,0:T(8,128)(2,1)}, bf16[32,16,256]{2,1,0:T(8,128)(2,1)}, u32[]{:S(2)}, u32[]{:S(2)}) collective-permute-start(bf16[32,16,256]{2,1,0:T(8,128)(2,1)} %slice_bitcast_fusion), channel_id=1, source_target_pairs={{0,384},{64,704},{128,512},{192,832},{256,640},{320,960},{384,768}... | collective-permute-start | bytes 786440 | tf_op jit(solution)/shard_map/ppermute | solution.py:167
  55.2 5.1 %collective-permute-start.5 = (bf16[2,32,16,256]{3,2,1,0:T(8,128)(2,1)S(1)}, bf16[2,32,16,256]{3,2,1,0:T(8,128)(2,1)S(1)}, u32[]{:S(2)}, u32[]{:S(2)}) collective-permute-start(bf16[2,32,16,256]{3,2,1,0:T(8,128)(2,1)S(1)} %collective-permute-done.2.refs_1_), channel_id=1, source_target_pairs={{0,64},{64,0},{128,192},{192,128},{256,320},{320,256},{384,448},{4... | collective-permute-start | bytes 1572872 | tf_op jit(solution)/shard_map/ppermute | solution.py:167
  60.3 1.9 %collective-permute-start.6 = (bf16[2,32,16,256]{3,2,1,0:T(8,128)(2,1)S(1)}, bf16[2,32,16,256]{3,2,1,0:T(8,128)(2,1)S(1)}, u32[]{:S(2)}, u32[]{:S(2)}) collective-permute-start(bf16[2,32,16,256]{3,2,1,0:T(8,128)(2,1)S(1)} %collective-permute-done.3.refs_2_), channel_id=1, source_target_pairs={{0,64},{64,0},{128,192},{192,128},{256,320},{320,256},{384,448},{4... | collective-permute-start | bytes 1572872 | tf_op jit(solution)/shard_map/ppermute | solution.py:167
  62.2 0.0 collective-permute-done.4.refs_3_
  62.2 2.4 %collective-permute-start.7 = (bf16[2,32,16,256]{3,2,1,0:T(8,128)(2,1)S(1)}, bf16[2,32,16,256]{3,2,1,0:T(8,128)(2,1)}, u32[]{:S(2)}, u32[]{:S(2)}) collective-permute-start(bf16[2,32,16,256]{3,2,1,0:T(8,128)(2,1)S(1)} %collective-permute-done.4.refs_3_), channel_id=1, source_target_pairs={{0,64},{64,0},{128,192},{192,128},{256,320},{320,256},{384,448},{4... | collective-permute-start | bytes 1572872 | tf_op jit(solution)/shard_map/ppermute | solution.py:167
  64.6 0.0 all-to-all-done.mine
  64.7 1.9 %collective-permute-start = (bf16[8,16,1024]{2,1,0:T(8,128)(2,1)S(1)}, bf16[8,16,1024]{2,1,0:T(8,128)(2,1)}, u32[]{:S(2)}, u32[]{:S(2)}) collective-permute-start(bf16[8,16,1024]{2,1,0:T(8,128)(2,1)S(1)} %all-to-all-done.mine), channel_id=1, source_target_pairs={{0,64},{64,0},{128,192},{192,128},{256,320},{320,256},{384,448},{4... | collective-permute-start | bytes 786440 | tf_op jit(solution)/shard_map/ppermute | solution.py:167
  66.6 0.0 collective-permute-done.8.refs_7_
  66.6 5.2 %collective-permute-start.9 = (bf16[32,16,256]{2,1,0:T(8,128)(2,1)}, bf16[32,16,256]{2,1,0:T(8,128)(2,1)S(1)}, u32[]{:S(2)}, u32[]{:S(2)}) collective-permute-start(bf16[32,16,256]{2,1,0:T(8,128)(2,1)} %collective-permute-done.8.refs_7_), channel_id=1, source_target_pairs={{0,64},{64,0},{128,192},{192,128},{256,320},{320,256},{384,448},{4... | collective-permute-start | bytes 786440 | tf_op jit(solution)/shard_map/ppermute | solution.py:167
  71.8 0.0 copy-start.6
  71.9 0.0 copy-start.5
  71.9 0.1 pad_add_fusion.where
  72.0 0.0 collective-permute-done.theirs
  72.0 0.0 copy-done.3
  72.0 0.6 copy-done.6
  72.5 0.0 copy-done.5
  72.6 0.1 copy-done.9
  72.6 5.9 %transform.1 = bf16[16,16,256]{2,1,0:T(8,128)(2,1)S(1)} custom-call(s32[3]{0:T(128)S(1)} %pad_add_fusion.where, bf16[8,16,1024]{2,1,0:T(8,128)(2,1)S(1)} %all-to-all-done.mine, bf16[8,16,1024]{2,1,0:T(8,128)(2,1)} %collective-permute-done.theirs, f32[8,128]{1,0:T(8,128)S(1)} %bitcast.13, f32[8,128]{1,0:T(8,128)S(1)} %bitcast.14, s32[16,512]{1,0:T(8,128)S(1)} %copy-done.3, ...), custom_call_target="tpu_custom_call" | custom-call | tf_op jit(solution)/shard_map/transform/pallas_call | solution.py:215
  78.5 0.0 copy-start.7
  78.5 0.0 copy-start.8
  78.5 15.0 %all_to_all.10.trans = bf16[16,16,256]{2,1,0:T(8,128)(2,1)S(1)} all-to-all(bf16[16,16,256]{2,1,0:T(8,128)(2,1)S(1)} %transform.1), channel_id=1, replica_groups=mesh['member'=16,'space'=64] {'member'}, dimensions={0} | all-to-all | bytes 262144 | tf_op jit(solution)/shard_map/all_to_all | solution.py:235
  93.5 0.0 collective-permute-done.9.refs_8_
  93.5 0.0 collective-permute-done.5.refs_4_
  93.5 0.0 collective-permute-done.6.refs_5_
  93.5 0.0 collective-permute-done.7.refs_6_
  93.5 0.0 copy-done.7
  93.6 0.0 copy-done.8
  93.6 3.9 %apply.1 = f32[16,32,256]{2,1,0:T(8,128)} custom-call(s32[3]{0:T(128)S(1)} %pad_add_fusion.where, bf16[16,16,256]{2,1,0:T(8,128)(2,1)S(1)} %all_to_all.10.trans, s32[4,256]{1,0:T(4,128)S(1)} %copy-done.7, f32[4,256]{1,0:T(4,128)S(1)} %copy-done.8, bf16[2,32,16,256]{3,2,1,0:T(8,128)(2,1)S(1)} %pad_maximum_fusion.refs_0_, ...), custom_call_target="tpu_custom_call" | custom-call | tf_op jit(solution)/shard_map/apply/pallas_call | solution.py:237
  (2 shorter events, 0.0 us)
Async XLA Ops:
  0.0 1.0 %copy-start = (f32[16,32,256]{2,1,0:T(8,128)S(1)}, f32[16,32,256]{2,1,0:T(8,128)}, u32[]{:S(2)}) copy-start(f32[16,32,256]{2,1,0:T(8,128)} %ens.3) | copy-start | bytes 1572868
  1.6 17.2 %collective-permute-start.1 = (bf16[32,16,256]{2,1,0:T(8,128)(2,1)S(1)}, bf16[32,16,256]{2,1,0:T(8,128)(2,1)S(1)}, u32[]{:S(2)}, u32[]{:S(2)}) collective-permute-start(bf16[32,16,256]{2,1,0:T(8,128)(2,1)S(1)} %pack.1), channel_id=1, source_target_pairs={{0,64},{64,0},{128,192},{192,128},{256,320},{320,256},{384,448},{4... | collective-permute-start | bytes 786440 | tf_op jit(solution)/shard_map/ppermute | solution.py:167
  18.7 24.4 %copy-start.1 = (f32[16,32,256]{2,1,0:T(8,128)S(1)}, f32[16,32,256]{2,1,0:T(8,128)}, u32[]{:S(2)}) copy-start(f32[16,32,256]{2,1,0:T(8,128)} %ens.3) | copy-start | bytes 1572868
  18.7 24.4 %copy-start.2 = (f32[32,1024]{1,0:T(8,128)S(1)}, f32[32,1024]{1,0:T(8,128)}, u32[]{:S(2)}) copy-start(f32[32,1024]{1,0:T(8,128)} %weight.1) | copy-start | bytes 393220
  18.7 24.4 %copy-start.4 = (s32[1024]{0:T(1024)S(1)}, s32[1024]{0:T(1024)}, u32[]{:S(2)}) copy-start(s32[1024]{0:T(1024)} %param.13) | copy-start | bytes 12292
  18.8 10.4 %collective-permute-start.2 = (bf16[2,32,16,256]{3,2,1,0:T(8,128)(2,1)S(1)}, bf16[2,32,16,256]{3,2,1,0:T(8,128)(2,1)S(1)}, u32[]{:S(2)}, u32[]{:S(2)}) collective-permute-start(bf16[2,32,16,256]{3,2,1,0:T(8,128)(2,1)S(1)} %pad_maximum_fusion.refs_0_), channel_id=1, source_target_pairs={{0,128},{64,960},{128,256},{192,64},{256,384},{320,192},{384,512},... | collective-permute-start | bytes 1572872 | tf_op jit(solution)/shard_map/ppermute | solution.py:167
  29.1 10.2 %collective-permute-start.3 = (bf16[2,32,16,256]{3,2,1,0:T(8,128)(2,1)S(1)}, bf16[2,32,16,256]{3,2,1,0:T(8,128)(2,1)S(1)}, u32[]{:S(2)}, u32[]{:S(2)}) collective-permute-start(bf16[2,32,16,256]{3,2,1,0:T(8,128)(2,1)S(1)} %collective-permute-done.2.refs_1_), channel_id=1, source_target_pairs={{0,128},{64,960},{128,256},{192,64},{256,384},{320,192},{384,512},... | collective-permute-start | bytes 1572872 | tf_op jit(solution)/shard_map/ppermute | solution.py:167
  39.4 22.9 %collective-permute-start.4 = (bf16[2,32,16,256]{3,2,1,0:T(8,128)(2,1)S(1)}, bf16[2,32,16,256]{3,2,1,0:T(8,128)(2,1)S(1)}, u32[]{:S(2)}, u32[]{:S(2)}) collective-permute-start(bf16[2,32,16,256]{3,2,1,0:T(8,128)(2,1)S(1)} %collective-permute-done.3.refs_2_), channel_id=1, source_target_pairs={{0,128},{64,960},{128,256},{192,64},{256,384},{320,192},{384,512},... | collective-permute-start | bytes 1572872 | tf_op jit(solution)/shard_map/ppermute | solution.py:167
  44.6 20.0 %all-to-all-start = ((bf16[8,16,1024]{2,1,0:T(8,128)(2,1)}), bf16[8,16,1024]{2,1,0:T(8,128)(2,1)S(1)}, u32[]{:S(2)}, u32[]{:S(2)}) async-start(bf16[8,16,1024]{2,1,0:T(8,128)(2,1)} %observe.1), calls=%async_computation | async-start | bytes 524288 | tf_op jit(solution)/shard_map/all_to_all | solution.py:212
  48.8 23.2 %copy-start.3 = (s32[16,512]{1,0:T(8,128)S(1)}, s32[16,512]{1,0:T(8,128)}, u32[]{:S(2)}) copy-start(s32[16,512]{1,0:T(8,128)} %rows.1) | copy-start | bytes 98308
  48.8 17.8 %collective-permute-start.8 = (bf16[32,16,256]{2,1,0:T(8,128)(2,1)}, bf16[32,16,256]{2,1,0:T(8,128)(2,1)}, u32[]{:S(2)}, u32[]{:S(2)}) collective-permute-start(bf16[32,16,256]{2,1,0:T(8,128)(2,1)} %slice_bitcast_fusion), channel_id=1, source_target_pairs={{0,384},{64,704},{128,512},{192,832},{256,640},{320,960},{384,768}... | collective-permute-start | bytes 786440 | tf_op jit(solution)/shard_map/ppermute | solution.py:167
  55.2 38.3 %collective-permute-start.5 = (bf16[2,32,16,256]{3,2,1,0:T(8,128)(2,1)S(1)}, bf16[2,32,16,256]{3,2,1,0:T(8,128)(2,1)S(1)}, u32[]{:S(2)}, u32[]{:S(2)}) collective-permute-start(bf16[2,32,16,256]{3,2,1,0:T(8,128)(2,1)S(1)} %collective-permute-done.2.refs_1_), channel_id=1, source_target_pairs={{0,64},{64,0},{128,192},{192,128},{256,320},{320,256},{384,448},{4... | collective-permute-start | bytes 1572872 | tf_op jit(solution)/shard_map/ppermute | solution.py:167
  60.3 33.2 %collective-permute-start.6 = (bf16[2,32,16,256]{3,2,1,0:T(8,128)(2,1)S(1)}, bf16[2,32,16,256]{3,2,1,0:T(8,128)(2,1)S(1)}, u32[]{:S(2)}, u32[]{:S(2)}) collective-permute-start(bf16[2,32,16,256]{3,2,1,0:T(8,128)(2,1)S(1)} %collective-permute-done.3.refs_2_), channel_id=1, source_target_pairs={{0,64},{64,0},{128,192},{192,128},{256,320},{320,256},{384,448},{4... | collective-permute-start | bytes 1572872 | tf_op jit(solution)/shard_map/ppermute | solution.py:167
  62.2 31.3 %collective-permute-start.7 = (bf16[2,32,16,256]{3,2,1,0:T(8,128)(2,1)S(1)}, bf16[2,32,16,256]{3,2,1,0:T(8,128)(2,1)}, u32[]{:S(2)}, u32[]{:S(2)}) collective-permute-start(bf16[2,32,16,256]{3,2,1,0:T(8,128)(2,1)S(1)} %collective-permute-done.4.refs_3_), channel_id=1, source_target_pairs={{0,64},{64,0},{128,192},{192,128},{256,320},{320,256},{384,448},{4... | collective-permute-start | bytes 1572872 | tf_op jit(solution)/shard_map/ppermute | solution.py:167
  64.7 7.3 %collective-permute-start = (bf16[8,16,1024]{2,1,0:T(8,128)(2,1)S(1)}, bf16[8,16,1024]{2,1,0:T(8,128)(2,1)}, u32[]{:S(2)}, u32[]{:S(2)}) collective-permute-start(bf16[8,16,1024]{2,1,0:T(8,128)(2,1)S(1)} %all-to-all-done.mine), channel_id=1, source_target_pairs={{0,64},{64,0},{128,192},{192,128},{256,320},{320,256},{384,448},{4... | collective-permute-start | bytes 786440 | tf_op jit(solution)/shard_map/ppermute | solution.py:167
  66.6 26.9 %collective-permute-start.9 = (bf16[32,16,256]{2,1,0:T(8,128)(2,1)}, bf16[32,16,256]{2,1,0:T(8,128)(2,1)S(1)}, u32[]{:S(2)}, u32[]{:S(2)}) collective-permute-start(bf16[32,16,256]{2,1,0:T(8,128)(2,1)} %collective-permute-done.8.refs_7_), channel_id=1, source_target_pairs={{0,64},{64,0},{128,192},{192,128},{256,320},{320,256},{384,448},{4... | collective-permute-start | bytes 786440 | tf_op jit(solution)/shard_map/ppermute | solution.py:167
  71.8 0.7 copy-start.6
  71.9 0.7 copy-start.5
  72.0 0.7 copy-start.9
  78.5 15.0 %copy-start.7 = (s32[4,256]{1,0:T(4,128)S(1)}, s32[4,256]{1,0:T(4,128)}, u32[]{:S(2)}) copy-start(s32[4,256]{1,0:T(4,128)} %neighbour.1) | copy-start | bytes 12292
  78.5 15.0 %copy-start.8 = (f32[4,256]{1,0:T(4,128)S(1)}, f32[4,256]{1,0:T(4,128)}, u32[]{:S(2)}) copy-start(f32[4,256]{1,0:T(4,128)} %interp.1) | copy-start | bytes 12292
where the time goes:
time: 98.2 us; the launch traced here: 97.5 us
  starting transfers between devices  51 us (52%)
  waiting for transfers between devices  16.8 us (17%)
  blocking collectives  15 us (15%)
  Pallas kernels  11.8 us (12%)
  local copies, waits for them, and re-layouts  2.45 us (2%)
    ppermute x10, starting transfers between devices, permute(): return lax.ppermute(value, 'member', pairs)  47.6 us
    ppermute x10, waiting for transfers between devices, permute(): return lax.ppermute(value, 'member', pairs)  16.8 us
    all_to_all x1, blocking collectives, analysis(): trans = lax.all_to_all(trans, 'member', 0, 0, tiled=True)  15 us
    pallas_call x1, Pallas kernels, analysis(): pl.pallas_call(transform_kernel, out_shape=jax.ShapeDtypeStruct((count, p...  5.9 us
    pallas_call x1, Pallas kernels, analysis(): pl.pallas_call(apply_kernel, out_shape=jax.ShapeDtypeStruct((per, nv, col...  3.91 us
    all_to_all x1, starting transfers between devices, analysis(): lax.all_to_all(seen, 'member', 0, 0, axis_index_groups=same_core, tiled=T...  3.41 us
  transfers between devices with their start and end apart: 11, of which 3 were waited for; matrix products, arithmetic and copies ran while one was open for 1% of the time, Pallas kernels for 8%

commit v1 on v0

--- a/solution.py
+++ b/solution.py
@@ -56,7 +56,7 @@
             out[chip, :, at] = seen
 
 
-def transform_kernel(where, mine, theirs, value, rinv, rows, counts, out, obs, scaled):
+def transform_kernel(where, mine, theirs, value, rinv, rows, out, obs, scaled):
     chips, per, n_obs = mine.shape
     size = chips * 2 * per
     me, core = where[0], where[1]
@@ -64,9 +64,7 @@
         obs[pl.ds(pl.multiple_of(2 * per * chip + per * core, per), per), :] = mine[chip]
         obs[pl.ds(pl.multiple_of(2 * per * chip + per * (1 - core), per), per), :] = theirs[chip]
     picks = rows[pl.ds(me, 1), :]
-    mine_only = lax.broadcasted_iota(jnp.int32, counts.shape, 1) == me
-    count = jnp.sum(jnp.where(mine_only, counts[...].astype(F32), 0.0), axis=1, keepdims=True)
-    live = lax.broadcasted_iota(jnp.int32, picks.shape, 1).astype(F32) < count
+    live = lax.broadcasted_iota(jnp.int32, picks.shape, 1) < where[3 + me]
     picks = jnp.where(live, picks, -1)
     tiles = n_obs // 128
     coarse = lax.broadcasted_iota(jnp.int32, (tiles, picks.shape[1]), 0) == (picks >> 7)
@@ -172,7 +170,7 @@
     chips = count // 2
     me = lax.axis_index("member").astype(jnp.int32)
     core = me % 2
-    where = jnp.stack([me, core, me // 2])
+    where = jnp.concatenate([jnp.stack([me, core, me // 2]), set_count])
     per, nv, cols = ensemble.shape
     n_obs = obs_column.shape[0]
     swap = [(i, i ^ 1) for i in range(count)]
@@ -215,7 +213,7 @@
     trans = pl.pallas_call(
         transform_kernel,
         out_shape=jax.ShapeDtypeStruct((count, per, count * per), BF16),
-        in_specs=[SMEM] + [VMEM] * 6,
+        in_specs=[SMEM] + [VMEM] * 5,
         out_specs=VMEM,
         scratch_shapes=[
             pltpu.VMEM((count * per, n_obs), BF16),
@@ -230,7 +228,6 @@
         obs_value.reshape(n_obs // 128, 128),
         obs_rinv.reshape(n_obs // 128, 128),
         set_rows,
-        set_count.reshape(1, count),
     )
     trans = lax.all_to_all(trans, "member", 0, 0, tiled=True)
 

time: 98.2 us -> 98.1 us (level)
  no operation moved by 1% of the time
where the time goes in v1:
time: 98.1 us; the launch traced here: 97.4 us
  starting transfers between devices  51 us (52%)
  waiting for transfers between devices  16.8 us (17%)
  blocking collectives  15 us (15%)
  Pallas kernels  11.7 us (12%)
  local copies, waits for them, and re-layouts  2.39 us (2%)
    ppermute x10, starting transfers between devices, permute(): return lax.ppermute(value, 'member', pairs)  47.6 us
    ppermute x10, waiting for transfers between devices, permute(): return lax.ppermute(value, 'member', pairs)  16.8 us
    all_to_all x1, blocking collectives, analysis(): trans = lax.all_to_all(trans, 'member', 0, 0, tiled=True)  15 us
    pallas_call x1, Pallas kernels, analysis(): pl.pallas_call(transform_kernel, out_shape=jax.ShapeDtypeStruct((count, p...  5.82 us
    pallas_call x1, Pallas kernels, analysis(): pl.pallas_call(apply_kernel, out_shape=jax.ShapeDtypeStruct((per, nv, col...  3.91 us
    all_to_all x1, starting transfers between devices, analysis(): lax.all_to_all(seen, 'member', 0, 0, axis_index_groups=same_core, tiled=T...  3.41 us
  transfers between devices with their start and end apart: 11, of which 3 were waited for; matrix products, arithmetic and copies ran while one was open for 1% of the time, Pallas kernels for 8%

profile of v1, /device:TPU:1, one launch (start us, length us, event | category | flops | bytes accessed | tf_op | source)
XLA Modules:
  0.0 97.4 jit_solution(14013494066785054557)
XLA Ops:
  0.0 0.0 copy-start
  0.0 1.0 %copy-done = f32[16,32,256]{2,1,0:T(8,128)S(1)} copy-done((f32[16,32,256]{2,1,0:T(8,128)S(1)}, f32[16,32,256]{2,1,0:T(8,128)}, u32[]{:S(2)}) %copy-start) | copy-done | bytes 524312
  1.0 0.5 pack.1
  1.6 16.0 %collective-permute-start.1 = (bf16[32,16,256]{2,1,0:T(8,128)(2,1)S(1)}, bf16[32,16,256]{2,1,0:T(8,128)(2,1)S(1)}, u32[]{:S(2)}, u32[]{:S(2)}) collective-permute-start(bf16[32,16,256]{2,1,0:T(8,128)(2,1)S(1)} %pack.1), channel_id=1, source_target_pairs={{0,64},{64,0},{128,192},{192,128},{256,320},{320,256},{384,448},{4... | collective-permute-start | bytes 786440 | tf_op jit(solution)/shard_map/ppermute | solution.py:165
  17.6 1.1 %collective-permute-done.1 = bf16[32,16,256]{2,1,0:T(8,128)(2,1)S(1)} collective-permute-done((bf16[32,16,256]{2,1,0:T(8,128)(2,1)S(1)}, bf16[32,16,256]{2,1,0:T(8,128)(2,1)S(1)}, u32[]{:S(2)}, u32[]{:S(2)}) %collective-permute-start.1) | collective-permute-done | bytes 262176 | tf_op jit(solution)/shard_map/ppermute | solution.py:165
  18.7 0.0 copy-start.1
  18.7 0.0 copy-start.2
  18.7 0.1 pad_maximum_fusion.refs_0_
  18.8 2.1 %collective-permute-start.2 = (bf16[2,32,16,256]{3,2,1,0:T(8,128)(2,1)S(1)}, bf16[2,32,16,256]{3,2,1,0:T(8,128)(2,1)S(1)}, u32[]{:S(2)}, u32[]{:S(2)}) collective-permute-start(bf16[2,32,16,256]{3,2,1,0:T(8,128)(2,1)S(1)} %pad_maximum_fusion.refs_0_), channel_id=1, source_target_pairs={{0,128},{64,960},{128,256},{192,64},{256,384},{320,192},{384,512},... | collective-permute-start | bytes 1572872 | tf_op jit(solution)/shard_map/ppermute | solution.py:165
  20.9 8.3 %collective-permute-done.2.refs_1_ = bf16[2,32,16,256]{3,2,1,0:T(8,128)(2,1)S(1)} collective-permute-done((bf16[2,32,16,256]{3,2,1,0:T(8,128)(2,1)S(1)}, bf16[2,32,16,256]{3,2,1,0:T(8,128)(2,1)S(1)}, u32[]{:S(2)}, u32[]{:S(2)}) %collective-permute-start.2) | collective-permute-done | bytes 524320 | tf_op jit(solution)/shard_map/ppermute | solution.py:165
  29.1 2.8 %collective-permute-start.3 = (bf16[2,32,16,256]{3,2,1,0:T(8,128)(2,1)S(1)}, bf16[2,32,16,256]{3,2,1,0:T(8,128)(2,1)S(1)}, u32[]{:S(2)}, u32[]{:S(2)}) collective-permute-start(bf16[2,32,16,256]{3,2,1,0:T(8,128)(2,1)S(1)} %collective-permute-done.2.refs_1_), channel_id=1, source_target_pairs={{0,128},{64,960},{128,256},{192,64},{256,384},{320,192},{384,512},... | collective-permute-start | bytes 1572872 | tf_op jit(solution)/shard_map/ppermute | solution.py:165
  32.0 7.4 %collective-permute-done.3.refs_2_ = bf16[2,32,16,256]{3,2,1,0:T(8,128)(2,1)S(1)} collective-permute-done((bf16[2,32,16,256]{3,2,1,0:T(8,128)(2,1)S(1)}, bf16[2,32,16,256]{3,2,1,0:T(8,128)(2,1)S(1)}, u32[]{:S(2)}, u32[]{:S(2)}) %collective-permute-start.3) | collective-permute-done | bytes 524320 | tf_op jit(solution)/shard_map/ppermute | solution.py:165
  39.4 3.7 %collective-permute-start.4 = (bf16[2,32,16,256]{3,2,1,0:T(8,128)(2,1)S(1)}, bf16[2,32,16,256]{3,2,1,0:T(8,128)(2,1)S(1)}, u32[]{:S(2)}, u32[]{:S(2)}) collective-permute-start(bf16[2,32,16,256]{3,2,1,0:T(8,128)(2,1)S(1)} %collective-permute-done.3.refs_2_), channel_id=1, source_target_pairs={{0,128},{64,960},{128,256},{192,64},{256,384},{320,192},{384,512},... | collective-permute-start | bytes 1572872 | tf_op jit(solution)/shard_map/ppermute | solution.py:165
  43.1 0.0 copy-done.1
  43.1 0.0 copy-done.2
  43.1 0.0 copy-done.4
  43.1 1.5 %observe.1 = bf16[8,16,1024]{2,1,0:T(8,128)(2,1)} custom-call(f32[16,32,256]{2,1,0:T(8,128)S(1)} %copy-done.1, f32[32,1024]{1,0:T(8,128)S(1)} %copy-done.2, s32[1,1024]{1,0:T(1,128)S(1)} %bitcast.11), custom_call_target="tpu_custom_call" | custom-call | tf_op jit(solution)/shard_map/observe/pallas_call | solution.py:202
  44.6 3.4 %all-to-all-start = ((bf16[8,16,1024]{2,1,0:T(8,128)(2,1)}), bf16[8,16,1024]{2,1,0:T(8,128)(2,1)S(1)}, u32[]{:S(2)}, u32[]{:S(2)}) async-start(bf16[8,16,1024]{2,1,0:T(8,128)(2,1)} %observe.1), calls=%async_computation | async-start | bytes 524288 | tf_op jit(solution)/shard_map/all_to_all | solution.py:210
  48.0 0.7 slice_bitcast_fusion
  48.8 6.4 %collective-permute-start.8 = (bf16[32,16,256]{2,1,0:T(8,128)(2,1)}, bf16[32,16,256]{2,1,0:T(8,128)(2,1)}, u32[]{:S(2)}, u32[]{:S(2)}) collective-permute-start(bf16[32,16,256]{2,1,0:T(8,128)(2,1)} %slice_bitcast_fusion), channel_id=1, source_target_pairs={{0,384},{64,704},{128,512},{192,832},{256,640},{320,960},{384,768}... | collective-permute-start | bytes 786440 | tf_op jit(solution)/shard_map/ppermute | solution.py:165
  55.2 5.1 %collective-permute-start.5 = (bf16[2,32,16,256]{3,2,1,0:T(8,128)(2,1)S(1)}, bf16[2,32,16,256]{3,2,1,0:T(8,128)(2,1)S(1)}, u32[]{:S(2)}, u32[]{:S(2)}) collective-permute-start(bf16[2,32,16,256]{3,2,1,0:T(8,128)(2,1)S(1)} %collective-permute-done.2.refs_1_), channel_id=1, source_target_pairs={{0,64},{64,0},{128,192},{192,128},{256,320},{320,256},{384,448},{4... | collective-permute-start | bytes 1572872 | tf_op jit(solution)/shard_map/ppermute | solution.py:165
  60.3 1.9 %collective-permute-start.6 = (bf16[2,32,16,256]{3,2,1,0:T(8,128)(2,1)S(1)}, bf16[2,32,16,256]{3,2,1,0:T(8,128)(2,1)S(1)}, u32[]{:S(2)}, u32[]{:S(2)}) collective-permute-start(bf16[2,32,16,256]{3,2,1,0:T(8,128)(2,1)S(1)} %collective-permute-done.3.refs_2_), channel_id=1, source_target_pairs={{0,64},{64,0},{128,192},{192,128},{256,320},{320,256},{384,448},{4... | collective-permute-start | bytes 1572872 | tf_op jit(solution)/shard_map/ppermute | solution.py:165
  62.2 0.0 collective-permute-done.4.refs_3_
  62.2 2.4 %collective-permute-start.7 = (bf16[2,32,16,256]{3,2,1,0:T(8,128)(2,1)S(1)}, bf16[2,32,16,256]{3,2,1,0:T(8,128)(2,1)}, u32[]{:S(2)}, u32[]{:S(2)}) collective-permute-start(bf16[2,32,16,256]{3,2,1,0:T(8,128)(2,1)S(1)} %collective-permute-done.4.refs_3_), channel_id=1, source_target_pairs={{0,64},{64,0},{128,192},{192,128},{256,320},{320,256},{384,448},{4... | collective-permute-start | bytes 1572872 | tf_op jit(solution)/shard_map/ppermute | solution.py:165
  64.6 0.0 all-to-all-done.mine
  64.7 1.9 %collective-permute-start = (bf16[8,16,1024]{2,1,0:T(8,128)(2,1)S(1)}, bf16[8,16,1024]{2,1,0:T(8,128)(2,1)}, u32[]{:S(2)}, u32[]{:S(2)}) collective-permute-start(bf16[8,16,1024]{2,1,0:T(8,128)(2,1)S(1)} %all-to-all-done.mine), channel_id=1, source_target_pairs={{0,64},{64,0},{128,192},{192,128},{256,320},{320,256},{384,448},{4... | collective-permute-start | bytes 786440 | tf_op jit(solution)/shard_map/ppermute | solution.py:165
  66.6 0.0 copy-start.9
  66.6 0.0 collective-permute-done.8.refs_7_
  66.6 5.2 %collective-permute-start.9 = (bf16[32,16,256]{2,1,0:T(8,128)(2,1)}, bf16[32,16,256]{2,1,0:T(8,128)(2,1)S(1)}, u32[]{:S(2)}, u32[]{:S(2)}) collective-permute-start(bf16[32,16,256]{2,1,0:T(8,128)(2,1)} %collective-permute-done.8.refs_7_), channel_id=1, source_target_pairs={{0,64},{64,0},{128,192},{192,128},{256,320},{320,256},{384,448},{4... | collective-permute-start | bytes 786440 | tf_op jit(solution)/shard_map/ppermute | solution.py:165
  71.8 0.0 copy-start.5
  71.9 0.0 copy-start.6
  71.9 0.0 copy-done.9
  71.9 0.1 pad_add_fusion.where
  72.0 0.0 collective-permute-done.theirs
  72.0 0.0 copy-done.3
  72.0 0.6 copy-done.5
  72.5 0.0 copy-done.6
  72.6 5.8 %transform.1 = bf16[16,16,256]{2,1,0:T(8,128)(2,1)S(1)} custom-call(s32[19]{0:T(128)S(1)} %pad_add_fusion.where, bf16[8,16,1024]{2,1,0:T(8,128)(2,1)S(1)} %all-to-all-done.mine, bf16[8,16,1024]{2,1,0:T(8,128)(2,1)} %collective-permute-done.theirs, f32[8,128]{1,0:T(8,128)S(1)} %bitcast.12, f32[8,128]{1,0:T(8,128)S(1)} %bitcast.13, s32[16,512]{1,0:T(8,128)S(1)} %copy-done.3), custom_call_target="tpu_custom_call" | custom-call | tf_op jit(solution)/shard_map/transform/pallas_call | solution.py:213
  78.4 0.0 copy-start.7
  78.4 0.0 copy-start.8
  78.4 15.0 %all_to_all.10.trans = bf16[16,16,256]{2,1,0:T(8,128)(2,1)S(1)} all-to-all(bf16[16,16,256]{2,1,0:T(8,128)(2,1)S(1)} %transform.1), channel_id=1, replica_groups=mesh['member'=16,'space'=64] {'member'}, dimensions={0} | all-to-all | bytes 262144 | tf_op jit(solution)/shard_map/all_to_all | solution.py:232
  93.4 0.0 collective-permute-done.9.refs_8_
  93.4 0.0 collective-permute-done.5.refs_4_
  93.4 0.0 collective-permute-done.6.refs_5_
  93.4 0.0 collective-permute-done.7.refs_6_
  93.4 0.0 copy-done.7
  93.4 0.0 copy-done.8
  93.4 3.9 %apply.1 = f32[16,32,256]{2,1,0:T(8,128)} custom-call(s32[19]{0:T(128)S(1)} %pad_add_fusion.where, bf16[16,16,256]{2,1,0:T(8,128)(2,1)S(1)} %all_to_all.10.trans, s32[4,256]{1,0:T(4,128)S(1)} %copy-done.7, f32[4,256]{1,0:T(4,128)S(1)} %copy-done.8, bf16[2,32,16,256]{3,2,1,0:T(8,128)(2,1)S(1)} %pad_maximum_fusion.refs_0_, ...), custom_call_target="tpu_custom_call" | custom-call | tf_op jit(solution)/shard_map/apply/pallas_call | solution.py:234
  (2 shorter events, 0.0 us)
Async XLA Ops:
  0.0 1.0 %copy-start = (f32[16,32,256]{2,1,0:T(8,128)S(1)}, f32[16,32,256]{2,1,0:T(8,128)}, u32[]{:S(2)}) copy-start(f32[16,32,256]{2,1,0:T(8,128)} %ens.3) | copy-start | bytes 1572868
  1.6 17.2 %collective-permute-start.1 = (bf16[32,16,256]{2,1,0:T(8,128)(2,1)S(1)}, bf16[32,16,256]{2,1,0:T(8,128)(2,1)S(1)}, u32[]{:S(2)}, u32[]{:S(2)}) collective-permute-start(bf16[32,16,256]{2,1,0:T(8,128)(2,1)S(1)} %pack.1), channel_id=1, source_target_pairs={{0,64},{64,0},{128,192},{192,128},{256,320},{320,256},{384,448},{4... | collective-permute-start | bytes 786440 | tf_op jit(solution)/shard_map/ppermute | solution.py:165
  18.7 24.4 %copy-start.1 = (f32[16,32,256]{2,1,0:T(8,128)S(1)}, f32[16,32,256]{2,1,0:T(8,128)}, u32[]{:S(2)}) copy-start(f32[16,32,256]{2,1,0:T(8,128)} %ens.3) | copy-start | bytes 1572868
  18.7 24.4 %copy-start.2 = (f32[32,1024]{1,0:T(8,128)S(1)}, f32[32,1024]{1,0:T(8,128)}, u32[]{:S(2)}) copy-start(f32[32,1024]{1,0:T(8,128)} %weight.1) | copy-start | bytes 393220
  18.7 24.4 %copy-start.4 = (s32[1024]{0:T(1024)S(1)}, s32[1024]{0:T(1024)}, u32[]{:S(2)}) copy-start(s32[1024]{0:T(1024)} %param.13) | copy-start | bytes 12292
  18.8 10.4 %collective-permute-start.2 = (bf16[2,32,16,256]{3,2,1,0:T(8,128)(2,1)S(1)}, bf16[2,32,16,256]{3,2,1,0:T(8,128)(2,1)S(1)}, u32[]{:S(2)}, u32[]{:S(2)}) collective-permute-start(bf16[2,32,16,256]{3,2,1,0:T(8,128)(2,1)S(1)} %pad_maximum_fusion.refs_0_), channel_id=1, source_target_pairs={{0,128},{64,960},{128,256},{192,64},{256,384},{320,192},{384,512},... | collective-permute-start | bytes 1572872 | tf_op jit(solution)/shard_map/ppermute | solution.py:165
  29.1 10.2 %collective-permute-start.3 = (bf16[2,32,16,256]{3,2,1,0:T(8,128)(2,1)S(1)}, bf16[2,32,16,256]{3,2,1,0:T(8,128)(2,1)S(1)}, u32[]{:S(2)}, u32[]{:S(2)}) collective-permute-start(bf16[2,32,16,256]{3,2,1,0:T(8,128)(2,1)S(1)} %collective-permute-done.2.refs_1_), channel_id=1, source_target_pairs={{0,128},{64,960},{128,256},{192,64},{256,384},{320,192},{384,512},... | collective-permute-start | bytes 1572872 | tf_op jit(solution)/shard_map/ppermute | solution.py:165
  39.4 22.9 %collective-permute-start.4 = (bf16[2,32,16,256]{3,2,1,0:T(8,128)(2,1)S(1)}, bf16[2,32,16,256]{3,2,1,0:T(8,128)(2,1)S(1)}, u32[]{:S(2)}, u32[]{:S(2)}) collective-permute-start(bf16[2,32,16,256]{3,2,1,0:T(8,128)(2,1)S(1)} %collective-permute-done.3.refs_2_), channel_id=1, source_target_pairs={{0,128},{64,960},{128,256},{192,64},{256,384},{320,192},{384,512},... | collective-permute-start | bytes 1572872 | tf_op jit(solution)/shard_map/ppermute | solution.py:165
  44.6 20.0 %all-to-all-start = ((bf16[8,16,1024]{2,1,0:T(8,128)(2,1)}), bf16[8,16,1024]{2,1,0:T(8,128)(2,1)S(1)}, u32[]{:S(2)}, u32[]{:S(2)}) async-start(bf16[8,16,1024]{2,1,0:T(8,128)(2,1)} %observe.1), calls=%async_computation | async-start | bytes 524288 | tf_op jit(solution)/shard_map/all_to_all | solution.py:210
  48.8 23.2 %copy-start.3 = (s32[16,512]{1,0:T(8,128)S(1)}, s32[16,512]{1,0:T(8,128)}, u32[]{:S(2)}) copy-start(s32[16,512]{1,0:T(8,128)} %rows.1) | copy-start | bytes 98308
  48.8 17.9 %collective-permute-start.8 = (bf16[32,16,256]{2,1,0:T(8,128)(2,1)}, bf16[32,16,256]{2,1,0:T(8,128)(2,1)}, u32[]{:S(2)}, u32[]{:S(2)}) collective-permute-start(bf16[32,16,256]{2,1,0:T(8,128)(2,1)} %slice_bitcast_fusion), channel_id=1, source_target_pairs={{0,384},{64,704},{128,512},{192,832},{256,640},{320,960},{384,768}... | collective-permute-start | bytes 786440 | tf_op jit(solution)/shard_map/ppermute | solution.py:165
  55.2 38.2 %collective-permute-start.5 = (bf16[2,32,16,256]{3,2,1,0:T(8,128)(2,1)S(1)}, bf16[2,32,16,256]{3,2,1,0:T(8,128)(2,1)S(1)}, u32[]{:S(2)}, u32[]{:S(2)}) collective-permute-start(bf16[2,32,16,256]{3,2,1,0:T(8,128)(2,1)S(1)} %collective-permute-done.2.refs_1_), channel_id=1, source_target_pairs={{0,64},{64,0},{128,192},{192,128},{256,320},{320,256},{384,448},{4... | collective-permute-start | bytes 1572872 | tf_op jit(solution)/shard_map/ppermute | solution.py:165
  60.3 33.1 %collective-permute-start.6 = (bf16[2,32,16,256]{3,2,1,0:T(8,128)(2,1)S(1)}, bf16[2,32,16,256]{3,2,1,0:T(8,128)(2,1)S(1)}, u32[]{:S(2)}, u32[]{:S(2)}) collective-permute-start(bf16[2,32,16,256]{3,2,1,0:T(8,128)(2,1)S(1)} %collective-permute-done.3.refs_2_), channel_id=1, source_target_pairs={{0,64},{64,0},{128,192},{192,128},{256,320},{320,256},{384,448},{4... | collective-permute-start | bytes 1572872 | tf_op jit(solution)/shard_map/ppermute | solution.py:165
  62.2 31.2 %collective-permute-start.7 = (bf16[2,32,16,256]{3,2,1,0:T(8,128)(2,1)S(1)}, bf16[2,32,16,256]{3,2,1,0:T(8,128)(2,1)}, u32[]{:S(2)}, u32[]{:S(2)}) collective-permute-start(bf16[2,32,16,256]{3,2,1,0:T(8,128)(2,1)S(1)} %collective-permute-done.4.refs_3_), channel_id=1, source_target_pairs={{0,64},{64,0},{128,192},{192,128},{256,320},{320,256},{384,448},{4... | collective-permute-start | bytes 1572872 | tf_op jit(solution)/shard_map/ppermute | solution.py:165
  64.7 7.3 %collective-permute-start = (bf16[8,16,1024]{2,1,0:T(8,128)(2,1)S(1)}, bf16[8,16,1024]{2,1,0:T(8,128)(2,1)}, u32[]{:S(2)}, u32[]{:S(2)}) collective-permute-start(bf16[8,16,1024]{2,1,0:T(8,128)(2,1)S(1)} %all-to-all-done.mine), channel_id=1, source_target_pairs={{0,64},{64,0},{128,192},{192,128},{256,320},{320,256},{384,448},{4... | collective-permute-start | bytes 786440 | tf_op jit(solution)/shard_map/ppermute | solution.py:165
  66.6 5.3 %copy-start.9 = (s32[16]{0:T(128)S(1)}, s32[16]{0:T(128)}, u32[]{:S(2)}) copy-start(s32[16]{0:T(128)} %param.15) | copy-start | bytes 196
  66.6 26.8 %collective-permute-start.9 = (bf16[32,16,256]{2,1,0:T(8,128)(2,1)}, bf16[32,16,256]{2,1,0:T(8,128)(2,1)S(1)}, u32[]{:S(2)}, u32[]{:S(2)}) collective-permute-start(bf16[32,16,256]{2,1,0:T(8,128)(2,1)} %collective-permute-done.8.refs_7_), channel_id=1, source_target_pairs={{0,64},{64,0},{128,192},{192,128},{256,320},{320,256},{384,448},{4... | collective-permute-start | bytes 786440 | tf_op jit(solution)/shard_map/ppermute | solution.py:165
  71.8 0.7 copy-start.5
  71.9 0.7 copy-start.6
  78.4 15.0 %copy-start.7 = (s32[4,256]{1,0:T(4,128)S(1)}, s32[4,256]{1,0:T(4,128)}, u32[]{:S(2)}) copy-start(s32[4,256]{1,0:T(4,128)} %neighbour.1) | copy-start | bytes 12292
  78.4 15.0 %copy-start.8 = (f32[4,256]{1,0:T(4,128)S(1)}, f32[4,256]{1,0:T(4,128)}, u32[]{:S(2)}) copy-start(f32[4,256]{1,0:T(4,128)} %interp.1) | copy-start | bytes 12292

commit v2 on v1

--- a/solution.py
+++ b/solution.py
@@ -112,9 +112,9 @@
 
 
 def apply_kernel(where, trans, neighbour, interp, *refs):
-    blocks, (out, lhs) = refs[:-2], refs[-2:]
+    blocks, (out, lhs, held, sems) = refs[:-4], refs[-4:]
     points, per, size = trans.shape
-    nv, cols = out.shape[1:]
+    nv, cols = held.shape[1:]
     core, chip = where[1], where[2]
     chips = size // (2 * per)
     raw = interp[...]
@@ -139,6 +139,7 @@
     shuffle = (lax.broadcasted_iota(jnp.int32, (size, size), 0) == column).astype(F32).astype(BF16)
     lhs[: points * per] = dot(flat, shuffle).astype(BF16)
     lhs[points * per :] = jnp.full((16, size), 1.0 / size, BF16)
+    each, copies = nv // sems.shape[0], []
     for v in range(nv):
         states = jnp.concatenate(
             [blocks[which][v] if index is None else blocks[which][index, v] for which, index, _, _ in slabs()], axis=0
@@ -147,7 +148,13 @@
         total = res[points * per : points * per + 1] * rest
         for m in range(points):
             total = total + res[per * m : per * (m + 1)] * pointwise[m : m + 1]
-        out[:, v, :] = total
+        held[:, v, :] = total
+        if (v + 1) % each == 0:
+            at = pl.ds(v + 1 - each, each)
+            copies.append(pltpu.make_async_copy(held.at[:, at], out.at[:, at], sems.at[len(copies)]))
+            copies[-1].start()
+    for copy in copies:
+        copy.wait()
 
 
 def slabs():
@@ -235,9 +242,11 @@
         apply_kernel,
         out_shape=jax.ShapeDtypeStruct((per, nv, cols), F32),
         in_specs=[SMEM] + [VMEM] * (3 + len(blocks)),
-        out_specs=VMEM,
+        out_specs=pl.BlockSpec(memory_space=pl.ANY),
         scratch_shapes=[
             pltpu.VMEM((count * per + 16, count * per), BF16),
+            pltpu.VMEM((per, nv, cols), F32),
+            pltpu.SemaphoreType.DMA((4,)),
         ],
         compiler_params=limit(4),
         name="apply",

time: 98.1 us -> 98 us (level)
  no operation moved by 1% of the time
where the time goes in v2:
time: 98 us; the launch traced here: 97.2 us
  starting transfers between devices  51 us (52%)
  waiting for transfers between devices  16.8 us (17%)
  blocking collectives  15 us (15%)
  Pallas kernels  11.6 us (12%)
  local copies, waits for them, and re-layouts  2.39 us (2%)
    ppermute x10, starting transfers between devices, permute(): return lax.ppermute(value, 'member', pairs)  47.6 us
    ppermute x10, waiting for transfers between devices, permute(): return lax.ppermute(value, 'member', pairs)  16.8 us
    all_to_all x1, blocking collectives, analysis(): trans = lax.all_to_all(trans, 'member', 0, 0, tiled=True)  15 us
    pallas_call x1, Pallas kernels, analysis(): pl.pallas_call(transform_kernel, out_shape=jax.ShapeDtypeStruct((count, p...  5.82 us
    pallas_call x1, Pallas kernels, analysis(): pl.pallas_call(apply_kernel, out_shape=jax.ShapeDtypeStruct((per, nv, col...  3.81 us
    all_to_all x1, starting transfers between devices, analysis(): lax.all_to_all(seen, 'member', 0, 0, axis_index_groups=same_core, tiled=T...  3.41 us
  transfers between devices with their start and end apart: 11, of which 3 were waited for; matrix products, arithmetic and copies ran while one was open for 1% of the time, Pallas kernels for 8%

profile of v2, /device:TPU:1, one launch (start us, length us, event | category | flops | bytes accessed | tf_op | source)
XLA Modules:
  0.0 97.2 jit_solution(9053562259249424975)
XLA Ops:
  0.0 0.0 copy-start
  0.0 1.0 %copy-done = f32[16,32,256]{2,1,0:T(8,128)S(1)} copy-done((f32[16,32,256]{2,1,0:T(8,128)S(1)}, f32[16,32,256]{2,1,0:T(8,128)}, u32[]{:S(2)}) %copy-start) | copy-done | bytes 524312
  1.0 0.5 pack.1
  1.6 16.0 %collective-permute-start.1 = (bf16[32,16,256]{2,1,0:T(8,128)(2,1)S(1)}, bf16[32,16,256]{2,1,0:T(8,128)(2,1)S(1)}, u32[]{:S(2)}, u32[]{:S(2)}) collective-permute-start(bf16[32,16,256]{2,1,0:T(8,128)(2,1)S(1)} %pack.1), channel_id=1, source_target_pairs={{0,64},{64,0},{128,192},{192,128},{256,320},{320,256},{384,448},{4... | collective-permute-start | bytes 786440 | tf_op jit(solution)/shard_map/ppermute | solution.py:172
  17.6 1.1 %collective-permute-done.1 = bf16[32,16,256]{2,1,0:T(8,128)(2,1)S(1)} collective-permute-done((bf16[32,16,256]{2,1,0:T(8,128)(2,1)S(1)}, bf16[32,16,256]{2,1,0:T(8,128)(2,1)S(1)}, u32[]{:S(2)}, u32[]{:S(2)}) %collective-permute-start.1) | collective-permute-done | bytes 262176 | tf_op jit(solution)/shard_map/ppermute | solution.py:172
  18.7 0.0 copy-start.1
  18.7 0.0 copy-start.2
  18.7 0.1 pad_maximum_fusion.refs_0_
  18.8 2.1 %collective-permute-start.2 = (bf16[2,32,16,256]{3,2,1,0:T(8,128)(2,1)S(1)}, bf16[2,32,16,256]{3,2,1,0:T(8,128)(2,1)S(1)}, u32[]{:S(2)}, u32[]{:S(2)}) collective-permute-start(bf16[2,32,16,256]{3,2,1,0:T(8,128)(2,1)S(1)} %pad_maximum_fusion.refs_0_), channel_id=1, source_target_pairs={{0,128},{64,960},{128,256},{192,64},{256,384},{320,192},{384,512},... | collective-permute-start | bytes 1572872 | tf_op jit(solution)/shard_map/ppermute | solution.py:172
  20.9 8.3 %collective-permute-done.2.refs_1_ = bf16[2,32,16,256]{3,2,1,0:T(8,128)(2,1)S(1)} collective-permute-done((bf16[2,32,16,256]{3,2,1,0:T(8,128)(2,1)S(1)}, bf16[2,32,16,256]{3,2,1,0:T(8,128)(2,1)S(1)}, u32[]{:S(2)}, u32[]{:S(2)}) %collective-permute-start.2) | collective-permute-done | bytes 524320 | tf_op jit(solution)/shard_map/ppermute | solution.py:172
  29.1 2.8 %collective-permute-start.3 = (bf16[2,32,16,256]{3,2,1,0:T(8,128)(2,1)S(1)}, bf16[2,32,16,256]{3,2,1,0:T(8,128)(2,1)S(1)}, u32[]{:S(2)}, u32[]{:S(2)}) collective-permute-start(bf16[2,32,16,256]{3,2,1,0:T(8,128)(2,1)S(1)} %collective-permute-done.2.refs_1_), channel_id=1, source_target_pairs={{0,128},{64,960},{128,256},{192,64},{256,384},{320,192},{384,512},... | collective-permute-start | bytes 1572872 | tf_op jit(solution)/shard_map/ppermute | solution.py:172
  32.0 7.4 %collective-permute-done.3.refs_2_ = bf16[2,32,16,256]{3,2,1,0:T(8,128)(2,1)S(1)} collective-permute-done((bf16[2,32,16,256]{3,2,1,0:T(8,128)(2,1)S(1)}, bf16[2,32,16,256]{3,2,1,0:T(8,128)(2,1)S(1)}, u32[]{:S(2)}, u32[]{:S(2)}) %collective-permute-start.3) | collective-permute-done | bytes 524320 | tf_op jit(solution)/shard_map/ppermute | solution.py:172
  39.4 3.7 %collective-permute-start.4 = (bf16[2,32,16,256]{3,2,1,0:T(8,128)(2,1)S(1)}, bf16[2,32,16,256]{3,2,1,0:T(8,128)(2,1)S(1)}, u32[]{:S(2)}, u32[]{:S(2)}) collective-permute-start(bf16[2,32,16,256]{3,2,1,0:T(8,128)(2,1)S(1)} %collective-permute-done.3.refs_2_), channel_id=1, source_target_pairs={{0,128},{64,960},{128,256},{192,64},{256,384},{320,192},{384,512},... | collective-permute-start | bytes 1572872 | tf_op jit(solution)/shard_map/ppermute | solution.py:172
  43.1 0.0 copy-done.1
  43.1 0.0 copy-done.2
  43.1 0.0 copy-done.4
  43.1 1.5 %observe.1 = bf16[8,16,1024]{2,1,0:T(8,128)(2,1)} custom-call(f32[16,32,256]{2,1,0:T(8,128)S(1)} %copy-done.1, f32[32,1024]{1,0:T(8,128)S(1)} %copy-done.2, s32[1,1024]{1,0:T(1,128)S(1)} %bitcast.11), custom_call_target="tpu_custom_call" | custom-call | tf_op jit(solution)/shard_map/observe/pallas_call | solution.py:209
  44.6 3.4 %all-to-all-start = ((bf16[8,16,1024]{2,1,0:T(8,128)(2,1)}), bf16[8,16,1024]{2,1,0:T(8,128)(2,1)S(1)}, u32[]{:S(2)}, u32[]{:S(2)}) async-start(bf16[8,16,1024]{2,1,0:T(8,128)(2,1)} %observe.1), calls=%async_computation | async-start | bytes 524288 | tf_op jit(solution)/shard_map/all_to_all | solution.py:217
  48.0 0.7 slice_bitcast_fusion
  48.8 6.4 %collective-permute-start.8 = (bf16[32,16,256]{2,1,0:T(8,128)(2,1)}, bf16[32,16,256]{2,1,0:T(8,128)(2,1)}, u32[]{:S(2)}, u32[]{:S(2)}) collective-permute-start(bf16[32,16,256]{2,1,0:T(8,128)(2,1)} %slice_bitcast_fusion), channel_id=1, source_target_pairs={{0,384},{64,704},{128,512},{192,832},{256,640},{320,960},{384,768}... | collective-permute-start | bytes 786440 | tf_op jit(solution)/shard_map/ppermute | solution.py:172
  55.2 5.1 %collective-permute-start.5 = (bf16[2,32,16,256]{3,2,1,0:T(8,128)(2,1)S(1)}, bf16[2,32,16,256]{3,2,1,0:T(8,128)(2,1)S(1)}, u32[]{:S(2)}, u32[]{:S(2)}) collective-permute-start(bf16[2,32,16,256]{3,2,1,0:T(8,128)(2,1)S(1)} %collective-permute-done.2.refs_1_), channel_id=1, source_target_pairs={{0,64},{64,0},{128,192},{192,128},{256,320},{320,256},{384,448},{4... | collective-permute-start | bytes 1572872 | tf_op jit(solution)/shard_map/ppermute | solution.py:172
  60.3 1.9 %collective-permute-start.6 = (bf16[2,32,16,256]{3,2,1,0:T(8,128)(2,1)S(1)}, bf16[2,32,16,256]{3,2,1,0:T(8,128)(2,1)S(1)}, u32[]{:S(2)}, u32[]{:S(2)}) collective-permute-start(bf16[2,32,16,256]{3,2,1,0:T(8,128)(2,1)S(1)} %collective-permute-done.3.refs_2_), channel_id=1, source_target_pairs={{0,64},{64,0},{128,192},{192,128},{256,320},{320,256},{384,448},{4... | collective-permute-start | bytes 1572872 | tf_op jit(solution)/shard_map/ppermute | solution.py:172
  62.2 0.0 collective-permute-done.4.refs_3_
  62.2 2.4 %collective-permute-start.7 = (bf16[2,32,16,256]{3,2,1,0:T(8,128)(2,1)S(1)}, bf16[2,32,16,256]{3,2,1,0:T(8,128)(2,1)}, u32[]{:S(2)}, u32[]{:S(2)}) collective-permute-start(bf16[2,32,16,256]{3,2,1,0:T(8,128)(2,1)S(1)} %collective-permute-done.4.refs_3_), channel_id=1, source_target_pairs={{0,64},{64,0},{128,192},{192,128},{256,320},{320,256},{384,448},{4... | collective-permute-start | bytes 1572872 | tf_op jit(solution)/shard_map/ppermute | solution.py:172
  64.6 0.0 all-to-all-done.mine
  64.7 1.9 %collective-permute-start = (bf16[8,16,1024]{2,1,0:T(8,128)(2,1)S(1)}, bf16[8,16,1024]{2,1,0:T(8,128)(2,1)}, u32[]{:S(2)}, u32[]{:S(2)}) collective-permute-start(bf16[8,16,1024]{2,1,0:T(8,128)(2,1)S(1)} %all-to-all-done.mine), channel_id=1, source_target_pairs={{0,64},{64,0},{128,192},{192,128},{256,320},{320,256},{384,448},{4... | collective-permute-start | bytes 786440 | tf_op jit(solution)/shard_map/ppermute | solution.py:172
  66.6 0.0 copy-start.9
  66.6 0.0 collective-permute-done.8.refs_7_
  66.6 5.2 %collective-permute-start.9 = (bf16[32,16,256]{2,1,0:T(8,128)(2,1)}, bf16[32,16,256]{2,1,0:T(8,128)(2,1)S(1)}, u32[]{:S(2)}, u32[]{:S(2)}) collective-permute-start(bf16[32,16,256]{2,1,0:T(8,128)(2,1)} %collective-permute-done.8.refs_7_), channel_id=1, source_target_pairs={{0,64},{64,0},{128,192},{192,128},{256,320},{320,256},{384,448},{4... | collective-permute-start | bytes 786440 | tf_op jit(solution)/shard_map/ppermute | solution.py:172
  71.8 0.0 copy-start.5
  71.9 0.0 copy-start.6
  71.9 0.0 copy-done.9
  71.9 0.1 pad_add_fusion.where
  72.0 0.0 collective-permute-done.theirs
  72.0 0.0 copy-done.3
  72.0 0.6 copy-done.5
  72.5 0.0 copy-done.6
  72.6 5.8 %transform.1 = bf16[16,16,256]{2,1,0:T(8,128)(2,1)S(1)} custom-call(s32[19]{0:T(128)S(1)} %pad_add_fusion.where, bf16[8,16,1024]{2,1,0:T(8,128)(2,1)S(1)} %all-to-all-done.mine, bf16[8,16,1024]{2,1,0:T(8,128)(2,1)} %collective-permute-done.theirs, f32[8,128]{1,0:T(8,128)S(1)} %bitcast.12, f32[8,128]{1,0:T(8,128)S(1)} %bitcast.13, s32[16,512]{1,0:T(8,128)S(1)} %copy-done.3), custom_call_target="tpu_custom_call" | custom-call | tf_op jit(solution)/shard_map/transform/pallas_call | solution.py:220
  78.4 0.0 copy-start.7
  78.4 0.0 copy-start.8
  78.4 15.0 %all_to_all.10.trans = bf16[16,16,256]{2,1,0:T(8,128)(2,1)S(1)} all-to-all(bf16[16,16,256]{2,1,0:T(8,128)(2,1)S(1)} %transform.1), channel_id=1, replica_groups=mesh['member'=16,'space'=64] {'member'}, dimensions={0} | all-to-all | bytes 262144 | tf_op jit(solution)/shard_map/all_to_all | solution.py:239
  93.4 0.0 collective-permute-done.9.refs_8_
  93.4 0.0 collective-permute-done.5.refs_4_
  93.4 0.0 collective-permute-done.6.refs_5_
  93.4 0.0 collective-permute-done.7.refs_6_
  93.4 0.0 copy-done.7
  93.4 0.0 copy-done.8
  93.4 3.8 %apply.1 = f32[16,32,256]{2,1,0:T(8,128)} custom-call(s32[19]{0:T(128)S(1)} %pad_add_fusion.where, bf16[16,16,256]{2,1,0:T(8,128)(2,1)S(1)} %all_to_all.10.trans, s32[4,256]{1,0:T(4,128)S(1)} %copy-done.7, f32[4,256]{1,0:T(4,128)S(1)} %copy-done.8, bf16[2,32,16,256]{3,2,1,0:T(8,128)(2,1)S(1)} %pad_maximum_fusion.refs_0_, ...), custom_call_target="tpu_custom_call" | custom-call | tf_op jit(solution)/shard_map/apply/pallas_call | solution.py:241
  (2 shorter events, 0.0 us)
Async XLA Ops:
  0.0 1.0 %copy-start = (f32[16,32,256]{2,1,0:T(8,128)S(1)}, f32[16,32,256]{2,1,0:T(8,128)}, u32[]{:S(2)}) copy-start(f32[16,32,256]{2,1,0:T(8,128)} %ens.3) | copy-start | bytes 1572868
  1.6 17.2 %collective-permute-start.1 = (bf16[32,16,256]{2,1,0:T(8,128)(2,1)S(1)}, bf16[32,16,256]{2,1,0:T(8,128)(2,1)S(1)}, u32[]{:S(2)}, u32[]{:S(2)}) collective-permute-start(bf16[32,16,256]{2,1,0:T(8,128)(2,1)S(1)} %pack.1), channel_id=1, source_target_pairs={{0,64},{64,0},{128,192},{192,128},{256,320},{320,256},{384,448},{4... | collective-permute-start | bytes 786440 | tf_op jit(solution)/shard_map/ppermute | solution.py:172
  18.7 24.4 %copy-start.1 = (f32[16,32,256]{2,1,0:T(8,128)S(1)}, f32[16,32,256]{2,1,0:T(8,128)}, u32[]{:S(2)}) copy-start(f32[16,32,256]{2,1,0:T(8,128)} %ens.3) | copy-start | bytes 1572868
  18.7 24.4 %copy-start.2 = (f32[32,1024]{1,0:T(8,128)S(1)}, f32[32,1024]{1,0:T(8,128)}, u32[]{:S(2)}) copy-start(f32[32,1024]{1,0:T(8,128)} %weight.1) | copy-start | bytes 393220
  18.7 24.4 %copy-start.4 = (s32[1024]{0:T(1024)S(1)}, s32[1024]{0:T(1024)}, u32[]{:S(2)}) copy-start(s32[1024]{0:T(1024)} %param.13) | copy-start | bytes 12292
  18.8 10.4 %collective-permute-start.2 = (bf16[2,32,16,256]{3,2,1,0:T(8,128)(2,1)S(1)}, bf16[2,32,16,256]{3,2,1,0:T(8,128)(2,1)S(1)}, u32[]{:S(2)}, u32[]{:S(2)}) collective-permute-start(bf16[2,32,16,256]{3,2,1,0:T(8,128)(2,1)S(1)} %pad_maximum_fusion.refs_0_), channel_id=1, source_target_pairs={{0,128},{64,960},{128,256},{192,64},{256,384},{320,192},{384,512},... | collective-permute-start | bytes 1572872 | tf_op jit(solution)/shard_map/ppermute | solution.py:172
  29.1 10.2 %collective-permute-start.3 = (bf16[2,32,16,256]{3,2,1,0:T(8,128)(2,1)S(1)}, bf16[2,32,16,256]{3,2,1,0:T(8,128)(2,1)S(1)}, u32[]{:S(2)}, u32[]{:S(2)}) collective-permute-start(bf16[2,32,16,256]{3,2,1,0:T(8,128)(2,1)S(1)} %collective-permute-done.2.refs_1_), channel_id=1, source_target_pairs={{0,128},{64,960},{128,256},{192,64},{256,384},{320,192},{384,512},... | collective-permute-start | bytes 1572872 | tf_op jit(solution)/shard_map/ppermute | solution.py:172
  39.4 22.9 %collective-permute-start.4 = (bf16[2,32,16,256]{3,2,1,0:T(8,128)(2,1)S(1)}, bf16[2,32,16,256]{3,2,1,0:T(8,128)(2,1)S(1)}, u32[]{:S(2)}, u32[]{:S(2)}) collective-permute-start(bf16[2,32,16,256]{3,2,1,0:T(8,128)(2,1)S(1)} %collective-permute-done.3.refs_2_), channel_id=1, source_target_pairs={{0,128},{64,960},{128,256},{192,64},{256,384},{320,192},{384,512},... | collective-permute-start | bytes 1572872 | tf_op jit(solution)/shard_map/ppermute | solution.py:172
  44.6 20.0 %all-to-all-start = ((bf16[8,16,1024]{2,1,0:T(8,128)(2,1)}), bf16[8,16,1024]{2,1,0:T(8,128)(2,1)S(1)}, u32[]{:S(2)}, u32[]{:S(2)}) async-start(bf16[8,16,1024]{2,1,0:T(8,128)(2,1)} %observe.1), calls=%async_computation | async-start | bytes 524288 | tf_op jit(solution)/shard_map/all_to_all | solution.py:217
  48.8 23.2 %copy-start.3 = (s32[16,512]{1,0:T(8,128)S(1)}, s32[16,512]{1,0:T(8,128)}, u32[]{:S(2)}) copy-start(s32[16,512]{1,0:T(8,128)} %rows.1) | copy-start | bytes 98308
  48.8 17.9 %collective-permute-start.8 = (bf16[32,16,256]{2,1,0:T(8,128)(2,1)}, bf16[32,16,256]{2,1,0:T(8,128)(2,1)}, u32[]{:S(2)}, u32[]{:S(2)}) collective-permute-start(bf16[32,16,256]{2,1,0:T(8,128)(2,1)} %slice_bitcast_fusion), channel_id=1, source_target_pairs={{0,384},{64,704},{128,512},{192,832},{256,640},{320,960},{384,768}... | collective-permute-start | bytes 786440 | tf_op jit(solution)/shard_map/ppermute | solution.py:172
  55.2 38.2 %collective-permute-start.5 = (bf16[2,32,16,256]{3,2,1,0:T(8,128)(2,1)S(1)}, bf16[2,32,16,256]{3,2,1,0:T(8,128)(2,1)S(1)}, u32[]{:S(2)}, u32[]{:S(2)}) collective-permute-start(bf16[2,32,16,256]{3,2,1,0:T(8,128)(2,1)S(1)} %collective-permute-done.2.refs_1_), channel_id=1, source_target_pairs={{0,64},{64,0},{128,192},{192,128},{256,320},{320,256},{384,448},{4... | collective-permute-start | bytes 1572872 | tf_op jit(solution)/shard_map/ppermute | solution.py:172
  60.3 33.1 %collective-permute-start.6 = (bf16[2,32,16,256]{3,2,1,0:T(8,128)(2,1)S(1)}, bf16[2,32,16,256]{3,2,1,0:T(8,128)(2,1)S(1)}, u32[]{:S(2)}, u32[]{:S(2)}) collective-permute-start(bf16[2,32,16,256]{3,2,1,0:T(8,128)(2,1)S(1)} %collective-permute-done.3.refs_2_), channel_id=1, source_target_pairs={{0,64},{64,0},{128,192},{192,128},{256,320},{320,256},{384,448},{4... | collective-permute-start | bytes 1572872 | tf_op jit(solution)/shard_map/ppermute | solution.py:172
  62.2 31.2 %collective-permute-start.7 = (bf16[2,32,16,256]{3,2,1,0:T(8,128)(2,1)S(1)}, bf16[2,32,16,256]{3,2,1,0:T(8,128)(2,1)}, u32[]{:S(2)}, u32[]{:S(2)}) collective-permute-start(bf16[2,32,16,256]{3,2,1,0:T(8,128)(2,1)S(1)} %collective-permute-done.4.refs_3_), channel_id=1, source_target_pairs={{0,64},{64,0},{128,192},{192,128},{256,320},{320,256},{384,448},{4... | collective-permute-start | bytes 1572872 | tf_op jit(solution)/shard_map/ppermute | solution.py:172
  64.7 7.3 %collective-permute-start = (bf16[8,16,1024]{2,1,0:T(8,128)(2,1)S(1)}, bf16[8,16,1024]{2,1,0:T(8,128)(2,1)}, u32[]{:S(2)}, u32[]{:S(2)}) collective-permute-start(bf16[8,16,1024]{2,1,0:T(8,128)(2,1)S(1)} %all-to-all-done.mine), channel_id=1, source_target_pairs={{0,64},{64,0},{128,192},{192,128},{256,320},{320,256},{384,448},{4... | collective-permute-start | bytes 786440 | tf_op jit(solution)/shard_map/ppermute | solution.py:172
  66.6 5.3 %copy-start.9 = (s32[16]{0:T(128)S(1)}, s32[16]{0:T(128)}, u32[]{:S(2)}) copy-start(s32[16]{0:T(128)} %param.15) | copy-start | bytes 196
  66.6 26.8 %collective-permute-start.9 = (bf16[32,16,256]{2,1,0:T(8,128)(2,1)}, bf16[32,16,256]{2,1,0:T(8,128)(2,1)S(1)}, u32[]{:S(2)}, u32[]{:S(2)}) collective-permute-start(bf16[32,16,256]{2,1,0:T(8,128)(2,1)} %collective-permute-done.8.refs_7_), channel_id=1, source_target_pairs={{0,64},{64,0},{128,192},{192,128},{256,320},{320,256},{384,448},{4... | collective-permute-start | bytes 786440 | tf_op jit(solution)/shard_map/ppermute | solution.py:172
  71.8 0.7 copy-start.5
  71.9 0.7 copy-start.6
  78.4 15.0 %copy-start.7 = (s32[4,256]{1,0:T(4,128)S(1)}, s32[4,256]{1,0:T(4,128)}, u32[]{:S(2)}) copy-start(s32[4,256]{1,0:T(4,128)} %neighbour.1) | copy-start | bytes 12292
  78.4 15.0 %copy-start.8 = (f32[4,256]{1,0:T(4,128)S(1)}, f32[4,256]{1,0:T(4,128)}, u32[]{:S(2)}) copy-start(f32[4,256]{1,0:T(4,128)} %interp.1) | copy-start | bytes 12292
